TPU v7x, 32 devices: a whole 2x2x4 slice. The times are simulated.
32 devices in a mesh: vessel: 2 (over core), gather: 16 (over z, y, x).
Axes of the slice: x: 2, y: 2, z: 4, core: 2. Of those that a mesh axis runs over, the one named last changes fastest.
Arguments:
- observed: bfloat16 [16, 16, 2048], P('gather'), may hold values from -6 to 6
- estimate: bfloat16 [2, 16, 16, 2048], P('vessel', 'gather'), may hold values from -6 to 6
- delays: int32 [2, 16], P('vessel', 'gather'), may hold values from 0 to 256
- taps_time: float32 [16, 7], replicated, may hold values from -2 to 2
- taps_shot: float32 [16, 7], replicated, may hold values from -0.5 to 0.5
- thresh: float32 [16], replicated, may hold values from 0.02 to 0.3
Outputs:
- deblended: bfloat16 [2, 16, 16, 2048], P('vessel', 'gather')
All inputs are finite; a program needn't handle non-finite values.
Results may differ from a plain program's by a relative error of at most 0.022.
Values may be sent and summed in bfloat16 or wider, within the bound.
A program may use at most 64 MiB of HBM per device.

v0:
```python
import jax
import jax.numpy as jnp
from jax import lax
from jax.sharding import PartitionSpec as P

TIME_SPACING = 4
SHOT_SPACING = 2
MAXD = 256
ITERS = 2


def late_shift(traces, shift_by):
    width = traces.shape[2]
    padded = jnp.pad(traces, ((0, 0), (0, 0), (MAXD, MAXD)))

    def late_single(trace, shift_amount):
        return lax.dynamic_slice_in_dim(trace, MAXD - shift_amount, width, 1)

    return jax.vmap(late_single)(padded, shift_by)


def early_shift(traces, shift_by):
    width = traces.shape[2]
    padded = jnp.pad(traces, ((0, 0), (0, 0), (MAXD, MAXD)))

    def early_single(trace, shift_amount):
        return lax.dynamic_slice_in_dim(trace, MAXD + shift_amount, width, 1)

    return jax.vmap(early_single)(padded, shift_by)


def along_time(field, taps, shift_sign):
    filter_reach = 3 * TIME_SPACING
    length = field.shape[3]
    padded = jnp.pad(field, ((0, 0), (0, 0), (0, 0), (filter_reach, filter_reach)))
    total = jnp.zeros((taps.shape[0],) + field.shape[1:], jnp.float32)
    for tap_index in range(-3, 4):
        start_offset = filter_reach + shift_sign * tap_index * TIME_SPACING
        total = (
            total
            + taps[:, tap_index + 3][:, None, None, None]
            * padded[:, :, :, start_offset : start_offset + length]
        )
    return total


def along_shots(field, taps, shift_sign):
    filter_reach = 3 * SHOT_SPACING
    length = field.shape[1]
    padded = jnp.pad(field, ((0, 0), (filter_reach, filter_reach), (0, 0), (0, 0)))
    total = jnp.zeros((taps.shape[0],) + field.shape[1:], jnp.float32)
    for tap_index in range(-3, 4):
        start_offset = filter_reach + shift_sign * tap_index * SHOT_SPACING
        total = (
            total
            + taps[:, tap_index + 3][:, None, None, None]
            * padded[:, start_offset : start_offset + length]
        )
    return total


def shrink_filter(plane, taps_time, taps_shot, thresh):
    field = plane.astype(jnp.float32)[None]
    group_time = taps_time.reshape(-1, 4, taps_time.shape[1])
    group_shot = taps_shot.reshape(-1, 4, taps_shot.shape[1])
    group_thresh = thresh.reshape(-1, 4)

    def channel(carry, pieces):
        time_taps, shot_taps, limits = pieces
        forward_pass = along_shots(along_time(field, time_taps, 1), shot_taps, 1)
        bound = limits[:, None, None, None]
        shrunk = forward_pass - jnp.clip(forward_pass, -bound, bound)
        back = along_time(along_shots(shrunk, shot_taps, -1), time_taps, -1)
        return (carry + jnp.sum(back, axis=0), None)

    total, _ = lax.scan(
        channel, jnp.zeros(plane.shape, jnp.float32), (group_time, group_shot, group_thresh)
    )
    return total.astype(jnp.bfloat16)


def pseudo_planes(current, observed, shot_delays):
    own = late_shift(current[0], shot_delays[0])
    blend = lax.psum(own, "vessel").astype(jnp.float32)
    resid = observed.astype(jnp.float32) - blend
    plane = current[0].astype(jnp.float32) + early_shift(resid, shot_delays[0])
    return plane.astype(jnp.bfloat16)[None]


def per_device(observed, estimate, delays, taps_time, taps_shot, thresh):
    current = estimate
    for step in range(ITERS):
        planes = pseudo_planes(current, observed, delays)
        filtered = jnp.stack(
            [
                shrink_filter(
                    lax.all_to_all(planes, "gather", split_axis=2, concat_axis=1, tiled=True)[0],
                    taps_time,
                    taps_shot,
                    thresh,
                )
            ]
        )
        current = lax.all_to_all(filtered, "gather", split_axis=1, concat_axis=2, tiled=True)
    return current


def solution(mesh):
    return jax.shard_map(
        per_device,
        mesh=mesh,
        in_specs=(
            P("gather", None, None),
            P("vessel", "gather", None, None),
            P("vessel", "gather"),
            P(),
            P(),
            P(),
        ),
        out_specs=P("vessel", "gather", None, None),
        check_vma=False,
    )
```

profile of v0, /device:TPU:0, one launch (start us, length us, event | category | flops | bytes accessed | tf_op | source)
XLA Modules:
  0.0 136.3 jit_solution(2640347895954889670)
XLA Ops:
  7.2 1.6 %pad_dynamic-slice_fusion.3 = bf16[1,16,2048]{2,1,0:T(8,128)(2,1)} fusion(s32[]{:T(128)} %bitcast.5, bf16[1,16,2048]{2,1,0:T(8,128)(2,1)} %bitcast.111), kind=kLoop, calls=%fused_computation.150 | loop fusion | bytes 131076 | tf_op jit(solution)/shard_map/vmap()/gather | solution.py:17
  8.8 21.3 %all-reduce.15.cloned.1.call-done = bf16[1,16,2048]{2,1,0:T(8,128)(2,1)} async-done(((bf16[1,16,2048]{2,1,0:T(8,128)(2,1)}), bf16[1,16,2048]{2,1,0:T(8,128)(2,1)}) %all-reduce.15.cloned.1.call-update) | async-done | bytes 65552 | tf_op jit(solution)/shard_map/psum | solution.py:84
  30.1 0.9 convert_subtract_fusion.1
  31.1 0.7 copy-done
  31.9 0.5 broadcast.734
  32.5 1.0 reduce.64
  33.5 0.7 reshape.633
  34.1 7.0 %all-to-all-start = ((bf16[16,2,1024]{2,1,0:T(2,128)(2,1)}), bf16[16,2,1024]{2,1,0:T(2,128)(2,1)S(1)}, u32[]{:S(2)}, u32[]{:S(2)}) async-start(bf16[16,2,1024]{2,1,0:T(2,128)(2,1)} %reshape.633), calls=%async_computation | async-start | bytes 131072 | tf_op jit(solution)/shard_map/all_to_all | solution.py:97
  41.2 0.6 copy-done.3
  41.9 0.6 copy-done.4
  42.6 6.0 %all-to-all-done = bf16[16,2,1024]{2,1,0:T(2,128)(2,1)S(1)} async-done(((bf16[16,2,1024]{2,1,0:T(2,128)(2,1)}), bf16[16,2,1024]{2,1,0:T(2,128)(2,1)S(1)}, u32[]{:S(2)}, u32[]{:S(2)}) %all-to-all-start) | async-done | bytes 65568 | tf_op jit(solution)/shard_map/all_to_all | solution.py:97
  48.9 12.3 %while.30 = (s32[]{:T(128)}, f32[16,1,2048]{2,0,1:T(8,128)S(1)}, f32[4,4,7]{2,1,0:T(4,128)S(1)}, f32[4,4,7]{2,1,0:T(4,128)S(1)}, f32[1,16,1,2048]{3,1,2,0:T(8,12...) while((s32[]{:T(128)}, f32[16,1,2048]{2,0,1:T(8,128)S(1)}, f32[4,4,7]{2,1,0:T(4,128)S(1)}, ...), condition=%wide.region_3.4_spmd.clone, body=%wide.region_1.3_spmd.clone.sunk | while | flops 7372807 | bytes 5506551 | solution.py:76
  50.0 0.5 minimum_subtract_fusion.4
  50.5 0.4 fusion.70
  51.0 0.9 add_reduce_fusion.4
  53.1 0.5 minimum_subtract_fusion.4
  53.6 0.4 fusion.70
  54.0 0.9 add_reduce_fusion.4
  56.1 0.5 minimum_subtract_fusion.4
  56.6 0.4 fusion.70
  57.1 0.9 add_reduce_fusion.4
  59.2 0.5 minimum_subtract_fusion.4
  60.2 0.9 add_reduce_fusion.4
  61.2 1.0 reduce.65
  62.2 10.1 %all_to_all.19 = bf16[16,2,1024]{2,1,0:T(2,128)(2,1)S(1)} all-to-all(bf16[16,2,1024]{2,1,0:T(2,128)(2,1)S(1)} %reshape.635), channel_id=1, replica_groups=mesh['vessel'=2,'gather'=16] {'gather'}, dimensions={0} | all-to-all | bytes 131072 | tf_op jit(solution)/shard_map/all_to_all | solution.py:104
  72.5 0.7 pad_dynamic-slice_fusion.2
  73.2 14.6 %all-reduce.17.cloned.1.call-done = bf16[1,16,2048]{2,1,0:T(8,128)(2,1)} async-done(((bf16[1,16,2048]{2,1,0:T(8,128)(2,1)}), bf16[1,16,2048]{2,1,0:T(8,128)(2,1)}) %all-reduce.17.cloned.1.call-update) | async-done | bytes 65552 | tf_op jit(solution)/shard_map/psum | solution.py:84
  87.8 0.9 convert_subtract_fusion
  89.0 1.0 reduce.66
  89.9 0.7 reshape.637
  90.6 6.8 %all-to-all-start.2 = ((bf16[16,2,1024]{2,1,0:T(2,128)(2,1)}), bf16[16,2,1024]{2,1,0:T(2,128)(2,1)S(1)}, u32[]{:S(2)}, u32[]{:S(2)}) async-start(bf16[16,2,1024]{2,1,0:T(2,128)(2,1)} %reshape.637), calls=%async_computation.2 | async-start | bytes 131072 | tf_op jit(solution)/shard_map/all_to_all | solution.py:97
  97.4 7.5 %all-to-all-done.2 = bf16[16,2,1024]{2,1,0:T(2,128)(2,1)S(1)} async-done(((bf16[16,2,1024]{2,1,0:T(2,128)(2,1)}), bf16[16,2,1024]{2,1,0:T(2,128)(2,1)S(1)}, u32[]{:S(2)}, u32[]{:S(2)}) %all-to-all-start.2) | async-done | bytes 65568 | tf_op jit(solution)/shard_map/all_to_all | solution.py:97
  105.2 12.3 %while.31 = (s32[]{:T(128)}, f32[16,1,2048]{2,0,1:T(8,128)S(1)}, f32[4,4,7]{2,1,0:T(4,128)S(1)}, f32[4,4,7]{2,1,0:T(4,128)S(1)}, f32[1,16,1,2048]{3,1,2,0:T(8,12...) while((s32[]{:T(128)}, f32[16,1,2048]{2,0,1:T(8,128)S(1)}, f32[4,4,7]{2,1,0:T(4,128)S(1)}, ...), condition=%wide.region_7.8_spmd.clone, body=%wide.region_5.7_spmd.clone.sunk | while | flops 7372807 | bytes 5506551 | solution.py:76
  106.3 0.5 minimum_subtract_fusion.5
  106.9 0.4 fusion.72
  107.3 0.9 add_reduce_fusion.5
  109.4 0.5 minimum_subtract_fusion.5
  109.9 0.4 fusion.72
  110.4 0.9 add_reduce_fusion.5
  112.5 0.5 minimum_subtract_fusion.5
  113.0 0.4 fusion.72
  113.4 0.9 add_reduce_fusion.5
  115.5 0.5 minimum_subtract_fusion.5
  116.1 0.4 fusion.72
  116.5 0.9 add_reduce_fusion.5
  117.6 1.0 reduce.67
  118.6 10.1 %all_to_all.40 = bf16[16,2,1024]{2,1,0:T(2,128)(2,1)S(1)} all-to-all(bf16[16,2,1024]{2,1,0:T(2,128)(2,1)S(1)} %reshape.639), channel_id=1, replica_groups=mesh['vessel'=2,'gather'=16] {'gather'}, dimensions={0} | all-to-all | bytes 131072 | tf_op jit(solution)/shard_map/all_to_all | solution.py:104
  128.8 0.7 copy.50
  (92 shorter events, 11.3 us)
Async XLA Ops:
  6.5 23.6 %all-reduce.15.cloned.1.call-start = ((), (), s32[]{:S(2)}) async-start(), calls=%async_computation.4 | async-start | bytes 131072 | tf_op jit(solution)/shard_map/psum | solution.py:84
  8.8 21.3 %copy-start.1 = (bf16[1,16,2048]{2,1,0:T(8,128)(2,1)S(1)}, bf16[1,16,2048]{2,1,0:T(8,128)(2,1)}, u32[]{:S(2)}) copy-start(bf16[1,16,2048]{2,1,0:T(8,128)(2,1)} %param.10) | copy-start | bytes 196612
  31.0 0.8 copy-start
  34.1 7.0 %copy-start.2 = (f32[16,7]{0,1:T(8,128)S(1)}, f32[16,7]{0,1:T(8,128)}, u32[]{:S(2)}) copy-start(f32[16,7]{0,1:T(8,128)} %param.13) | copy-start | bytes 1348
  34.1 14.5 %all-to-all-start = ((bf16[16,2,1024]{2,1,0:T(2,128)(2,1)}), bf16[16,2,1024]{2,1,0:T(2,128)(2,1)S(1)}, u32[]{:S(2)}, u32[]{:S(2)}) async-start(bf16[16,2,1024]{2,1,0:T(2,128)(2,1)} %reshape.633), calls=%async_computation | async-start | bytes 131072 | tf_op jit(solution)/shard_map/all_to_all | solution.py:97
  41.1 46.7 %all-reduce.17.cloned.1.call-start = ((), (), s32[]{:S(2)}) async-start(), calls=%async_computation.5 | async-start | bytes 131072 | tf_op jit(solution)/shard_map/psum | solution.py:84
  41.2 0.7 copy-start.3
  41.8 0.7 copy-start.4
  90.6 14.4 %all-to-all-start.2 = ((bf16[16,2,1024]{2,1,0:T(2,128)(2,1)}), bf16[16,2,1024]{2,1,0:T(2,128)(2,1)S(1)}, u32[]{:S(2)}, u32[]{:S(2)}) async-start(bf16[16,2,1024]{2,1,0:T(2,128)(2,1)} %reshape.637), calls=%async_computation.2 | async-start | bytes 131072 | tf_op jit(solution)/shard_map/all_to_all | solution.py:97
Sparse Core Ops, SparseCore 0:
  9.6 20.4 all-reduce.14
  73.3 14.4 all-reduce.16
where the time goes:
time: 137 us; the launch traced here: 136 us
  waiting for transfers between devices  49.5 us (36%)
  other arithmetic  23.8 us (17%)
  blocking collectives  20.2 us (15%)
  between operations  14.3 us (10%)
  local copies, waits for them, and re-layouts  14.1 us (10%)
  starting transfers between devices  13.8 us (10%)
    psum x2, waiting for transfers between devices, pseudo_planes(): blend = lax.psum(own, 'vessel').astype(jnp.float32)  35.9 us
    all_to_all x2, blocking collectives, per_device(): lax.all_to_all(filtered, 'gather', split_axis=1, concat_axis=2, tiled=True)  20.2 us
    all_to_all x2, starting transfers between devices, per_device(): lax.all_to_all(planes, 'gather', split_axis=2, concat_axis=1, tiled=True)[0]  13.8 us
    all_to_all x2, waiting for transfers between devices, per_device(): lax.all_to_all(planes, 'gather', split_axis=2, concat_axis=1, tiled=True)[0]  13.6 us
    reduce_sum x8, other arithmetic, channel(): return (carry + jnp.sum(back, axis=0), None)  7.3 us
    unnamed x26, local copies, waits for them, and re-layouts  5.08 us
    unnamed x8, other arithmetic  4.17 us
    sub x8, other arithmetic, channel(): shrunk = forward_pass - jnp.clip(forward_pass, -bound, bound)  4.06 us
  transfers between devices with their start and end apart: 4, of which 4 were waited for; matrix products, arithmetic and copies ran while one was open for 0% of the time, Pallas kernels for 0%

commit v1 on v0

--- a/solution.py
+++ b/solution.py
@@ -81,7 +81,7 @@
 
 def pseudo_planes(current, observed, shot_delays):
     own = late_shift(current[0], shot_delays[0])
-    blend = lax.psum(own, "vessel").astype(jnp.float32)
+    blend = jnp.sum(lax.all_gather(own, "vessel"), axis=0).astype(jnp.float32)
     resid = observed.astype(jnp.float32) - blend
     plane = current[0].astype(jnp.float32) + early_shift(resid, shot_delays[0])
     return plane.astype(jnp.bfloat16)[None]

time: 137 us -> 87.9 us (0.64)
  waiting for transfers between devices: 49.5 us -> 13.6 us
  between operations: 14.3 us -> 0.92 us
  blocking collectives: 20.2 us -> 24.2 us
  starting transfers between devices: 13.8 us -> 11.8 us
    psum x2 -> x0, waiting for transfers between devices: 35.9 us -> none  [pseudo_planes(): blend = lax.psum(own, 'vessel').astype(jnp.float32)]
    all_gather x0 -> x2, blocking collectives: none -> 3.93 us  [pseudo_planes(): blend = jnp.sum(lax.all_gather(own, 'vessel'), axis=0).astype(jnp.float32)]
    all_to_all x2, starting transfers between devices: 13.8 us -> 11.8 us  [per_device(): lax.all_to_all(planes, 'gather', split_axis=2, concat_axis=1, tiled=True)[0]]
    sub x2, other arithmetic: 1.71 us -> 0.03 us  [pseudo_planes(): resid = observed.astype(jnp.float32) - blend]
    unnamed x26 -> x25, local copies, waits for them, and re-layouts: 5.08 us -> 5.87 us
  transfers between devices with their start and end apart: 4 -> 2, of which waited for: 4 -> 2; matrix products, arithmetic and copies ran while one was open for 0% -> 0% of each run, Pallas kernels for 0% -> 0%
where the time goes in v1:
time: 87.9 us; the launch traced here: 87.3 us
  blocking collectives  24.2 us (28%)
  other arithmetic  22.5 us (26%)
  local copies, waits for them, and re-layouts  13.7 us (16%)
  waiting for transfers between devices  13.6 us (15%)
  starting transfers between devices  11.8 us (13%)
  between operations  0.92 us (1%)
    all_to_all x2, blocking collectives, per_device(): lax.all_to_all(filtered, 'gather', split_axis=1, concat_axis=2, tiled=True)  20.2 us
    all_to_all x2, waiting for transfers between devices, per_device(): lax.all_to_all(planes, 'gather', split_axis=2, concat_axis=1, tiled=True)[0]  13.6 us
    all_to_all x2, starting transfers between devices, per_device(): lax.all_to_all(planes, 'gather', split_axis=2, concat_axis=1, tiled=True)[0]  11.8 us
    reduce_sum x8, other arithmetic, channel(): return (carry + jnp.sum(back, axis=0), None)  7.3 us
    unnamed x25, local copies, waits for them, and re-layouts  5.87 us
    unnamed x8, other arithmetic  4.49 us
    sub x8, other arithmetic, channel(): shrunk = forward_pass - jnp.clip(forward_pass, -bound, bound)  4.06 us
    all_gather x2, blocking collectives, pseudo_planes(): blend = jnp.sum(lax.all_gather(own, 'vessel'), axis=0).astype(jnp.float32)  3.93 us
  transfers between devices with their start and end apart: 2, of which 2 were waited for; matrix products, arithmetic and copies ran while one was open for 0% of the time, Pallas kernels for 0%

profile of v1, /device:TPU:0, one launch (start us, length us, event | category | flops | bytes accessed | tf_op | source)
XLA Modules:
  0.0 87.3 jit_solution(6357473869587097281)
XLA Ops:
  0.7 0.9 %pad_dynamic-slice_fusion.3 = bf16[1,16,2048]{2,1,0:T(8,128)(2,1)S(1)} fusion(s32[]{:T(128)} %bitcast.5, bf16[1,16,2048]{2,1,0:T(8,128)(2,1)} %bitcast.123), kind=kLoop, calls=%fused_computation.151 | loop fusion | bytes 131076 | tf_op jit(solution)/shard_map/vmap()/gather | solution.py:17
  1.6 2.0 %all-gather = bf16[2,16,2048]{2,1,0:T(8,128)(2,1)S(1)} all-gather(bf16[1,16,2048]{2,1,0:T(8,128)(2,1)S(1)} %pad_dynamic-slice_fusion.3), channel_id=2, replica_groups=mesh['vessel'=2,'gather'=16] {'vessel'}, dimensions={0}, use_global_device_ids=true | all-gather | bytes 196608 | tf_op jit(solution)/shard_map/all_gather | solution.py:84
  3.7 0.8 copy-done.1
  4.6 0.7 copy-done
  5.5 0.6 broadcast.734
  6.1 1.0 %reduce.72 = bf16[16,2048]{1,0:T(8,128)(2,1)S(1)} reduce(bf16[16,1,1,2048]{3,2,1,0:T(2,128)(2,1)S(1)} %fusion.64, bf16[]{:T(256)} %broadcast.734), dimensions={1,2}, to_apply=%fusion.64.reduce_sub_computation | reduce | bytes 131074
  7.1 0.7 reshape.661
  7.8 8.3 %all-to-all-start = ((bf16[16,2,1024]{2,1,0:T(2,128)(2,1)}), bf16[16,2,1024]{2,1,0:T(2,128)(2,1)S(1)}, u32[]{:S(2)}, u32[]{:S(2)}) async-start(bf16[16,2,1024]{2,1,0:T(2,128)(2,1)} %reshape.661), calls=%async_computation | async-start | bytes 131072 | tf_op jit(solution)/shard_map/all_to_all | solution.py:97
  16.2 0.6 copy-done.3
  16.9 0.6 copy-done.4
  17.6 6.1 %all-to-all-done = bf16[16,2,1024]{2,1,0:T(2,128)(2,1)S(1)} async-done(((bf16[16,2,1024]{2,1,0:T(2,128)(2,1)}), bf16[16,2,1024]{2,1,0:T(2,128)(2,1)S(1)}, u32[]{:S(2)}, u32[]{:S(2)}) %all-to-all-start) | async-done | bytes 65568 | tf_op jit(solution)/shard_map/all_to_all | solution.py:97
  23.9 12.3 %while.30 = (s32[]{:T(128)}, f32[16,1,2048]{2,0,1:T(8,128)S(1)}, f32[4,4,7]{2,1,0:T(4,128)S(1)}, f32[4,4,7]{2,1,0:T(4,128)S(1)}, f32[1,16,1,2048]{3,1,2,0:T(8,12...) while((s32[]{:T(128)}, f32[16,1,2048]{2,0,1:T(8,128)S(1)}, f32[4,4,7]{2,1,0:T(4,128)S(1)}, ...), condition=%wide.region_3.4_spmd.clone, body=%wide.region_1.3_spmd.clone.sunk | while | flops 7372807 | bytes 5506551 | solution.py:76
  24.5 0.3 multiply_add_fusion.4
  25.0 0.5 minimum_subtract_fusion.4
  25.6 0.4 fusion.71
  26.0 0.9 %add_reduce_fusion.4 = f32[16,2048]{1,0:T(8,128)S(1)} fusion(f32[4,16,1,2048]{3,1,2,0:T(8,128)S(1)} %fusion.71, f32[4]{0:T(128)S(1)} %get-tuple-element.497, f32[4]{0:T(128)S(1)} %get-tuple-element.499, f32[4]{0:T(128)S(1)} %get-tuple-element.501, f32[4]{0:T(128)S(1)} %get-tuple-element.502, f32[4]{0:T(128)S(1)} %get-tuple-element.504, ...), kind=kLoop, calls=%fused_computation.36.clone.1 | loop fusion | flops 1802240 | bytes 655472 | tf_op jit(solution)/shard_map/while/body/eval_jaxpr/reduce_sum | solution.py:74
  28.1 0.5 minimum_subtract_fusion.4
  28.6 0.4 fusion.71
  29.1 0.9 %add_reduce_fusion.4 = f32[16,2048]{1,0:T(8,128)S(1)} fusion(f32[4,16,1,2048]{3,1,2,0:T(8,128)S(1)} %fusion.71, f32[4]{0:T(128)S(1)} %get-tuple-element.497, f32[4]{0:T(128)S(1)} %get-tuple-element.499, f32[4]{0:T(128)S(1)} %get-tuple-element.501, f32[4]{0:T(128)S(1)} %get-tuple-element.502, f32[4]{0:T(128)S(1)} %get-tuple-element.504, ...), kind=kLoop, calls=%fused_computation.36.clone.1 | loop fusion | flops 1802240 | bytes 655472 | tf_op jit(solution)/shard_map/while/body/eval_jaxpr/reduce_sum | solution.py:74
  31.2 0.5 minimum_subtract_fusion.4
  31.7 0.4 fusion.71
  32.1 0.9 %add_reduce_fusion.4 = f32[16,2048]{1,0:T(8,128)S(1)} fusion(f32[4,16,1,2048]{3,1,2,0:T(8,128)S(1)} %fusion.71, f32[4]{0:T(128)S(1)} %get-tuple-element.497, f32[4]{0:T(128)S(1)} %get-tuple-element.499, f32[4]{0:T(128)S(1)} %get-tuple-element.501, f32[4]{0:T(128)S(1)} %get-tuple-element.502, f32[4]{0:T(128)S(1)} %get-tuple-element.504, ...), kind=kLoop, calls=%fused_computation.36.clone.1 | loop fusion | flops 1802240 | bytes 655472 | tf_op jit(solution)/shard_map/while/body/eval_jaxpr/reduce_sum | solution.py:74
  34.2 0.5 minimum_subtract_fusion.4
  34.8 0.4 fusion.71
  35.2 0.9 %add_reduce_fusion.4 = f32[16,2048]{1,0:T(8,128)S(1)} fusion(f32[4,16,1,2048]{3,1,2,0:T(8,128)S(1)} %fusion.71, f32[4]{0:T(128)S(1)} %get-tuple-element.497, f32[4]{0:T(128)S(1)} %get-tuple-element.499, f32[4]{0:T(128)S(1)} %get-tuple-element.501, f32[4]{0:T(128)S(1)} %get-tuple-element.502, f32[4]{0:T(128)S(1)} %get-tuple-element.504, ...), kind=kLoop, calls=%fused_computation.36.clone.1 | loop fusion | flops 1802240 | bytes 655472 | tf_op jit(solution)/shard_map/while/body/eval_jaxpr/reduce_sum | solution.py:74
  36.3 1.0 %reduce.73 = bf16[16,2048]{1,0:T(8,128)(2,1)S(1)} reduce(bf16[16,1,1,2048]{3,2,1,0:T(2,128)(2,1)S(1)} %bitcast.121, bf16[]{:T(256)} %broadcast.734), dimensions={1,2}, to_apply=%bitcast.100.reduce_sub_computation | reduce | bytes 131074
  37.4 10.1 %all_to_all.19 = bf16[16,2,1024]{2,1,0:T(2,128)(2,1)S(1)} all-to-all(bf16[16,2,1024]{2,1,0:T(2,128)(2,1)S(1)} %reshape.663), channel_id=1, replica_groups=mesh['vessel'=2,'gather'=16] {'gather'}, dimensions={0} | all-to-all | bytes 131072 | tf_op jit(solution)/shard_map/all_to_all | solution.py:104
  47.7 1.9 %all-gather.1 = bf16[2,16,2048]{2,1,0:T(8,128)(2,1)S(1)} all-gather(bf16[1,16,2048]{2,1,0:T(8,128)(2,1)S(1)} %pad_dynamic-slice_fusion.2), channel_id=3, replica_groups=mesh['vessel'=2,'gather'=16] {'vessel'}, dimensions={0}, use_global_device_ids=true | all-gather | bytes 196608 | tf_op jit(solution)/shard_map/all_gather | solution.py:84
  50.0 1.0 %reduce.74 = bf16[16,2048]{1,0:T(8,128)(2,1)S(1)} reduce(bf16[16,1,1,2048]{3,2,1,0:T(2,128)(2,1)S(1)} %fusion.65, bf16[]{:T(256)} %broadcast.734), dimensions={1,2}, to_apply=%fusion.65.reduce_sub_computation | reduce | bytes 131074
  51.0 0.7 reshape.665
  51.7 3.5 %all-to-all-start.2 = ((bf16[16,2,1024]{2,1,0:T(2,128)(2,1)}), bf16[16,2,1024]{2,1,0:T(2,128)(2,1)S(1)}, u32[]{:S(2)}, u32[]{:S(2)}) async-start(bf16[16,2,1024]{2,1,0:T(2,128)(2,1)} %reshape.665), calls=%async_computation.2 | async-start | bytes 131072 | tf_op jit(solution)/shard_map/all_to_all | solution.py:97
  55.2 7.5 %all-to-all-done.2 = bf16[16,2,1024]{2,1,0:T(2,128)(2,1)S(1)} async-done(((bf16[16,2,1024]{2,1,0:T(2,128)(2,1)}), bf16[16,2,1024]{2,1,0:T(2,128)(2,1)S(1)}, u32[]{:S(2)}, u32[]{:S(2)}) %all-to-all-start.2) | async-done | bytes 65568 | tf_op jit(solution)/shard_map/all_to_all | solution.py:97
  63.0 12.3 %while.31 = (s32[]{:T(128)}, f32[16,1,2048]{2,0,1:T(8,128)S(1)}, f32[4,4,7]{2,1,0:T(4,128)S(1)}, f32[4,4,7]{2,1,0:T(4,128)S(1)}, f32[1,16,1,2048]{3,1,2,0:T(8,12...) while((s32[]{:T(128)}, f32[16,1,2048]{2,0,1:T(8,128)S(1)}, f32[4,4,7]{2,1,0:T(4,128)S(1)}, ...), condition=%wide.region_7.8_spmd.clone, body=%wide.region_5.7_spmd.clone.sunk | while | flops 7372807 | bytes 5506551 | solution.py:76
  64.1 0.5 minimum_subtract_fusion.5
  64.6 0.4 fusion.73
  65.0 0.9 %add_reduce_fusion.5 = f32[16,2048]{1,0:T(8,128)S(1)} fusion(f32[4,16,1,2048]{3,1,2,0:T(8,128)S(1)} %fusion.73, f32[4]{0:T(128)S(1)} %get-tuple-element.527, f32[4]{0:T(128)S(1)} %get-tuple-element.529, f32[4]{0:T(128)S(1)} %get-tuple-element.531, f32[4]{0:T(128)S(1)} %get-tuple-element.532, f32[4]{0:T(128)S(1)} %get-tuple-element.534, ...), kind=kLoop, calls=%fused_computation.105.clone.1 | loop fusion | flops 1802240 | bytes 655472 | tf_op jit(solution)/shard_map/while/body/eval_jaxpr/reduce_sum | solution.py:74
  67.2 0.5 minimum_subtract_fusion.5
  67.7 0.4 fusion.73
  68.1 0.9 %add_reduce_fusion.5 = f32[16,2048]{1,0:T(8,128)S(1)} fusion(f32[4,16,1,2048]{3,1,2,0:T(8,128)S(1)} %fusion.73, f32[4]{0:T(128)S(1)} %get-tuple-element.527, f32[4]{0:T(128)S(1)} %get-tuple-element.529, f32[4]{0:T(128)S(1)} %get-tuple-element.531, f32[4]{0:T(128)S(1)} %get-tuple-element.532, f32[4]{0:T(128)S(1)} %get-tuple-element.534, ...), kind=kLoop, calls=%fused_computation.105.clone.1 | loop fusion | flops 1802240 | bytes 655472 | tf_op jit(solution)/shard_map/while/body/eval_jaxpr/reduce_sum | solution.py:74
  70.2 0.5 minimum_subtract_fusion.5
  70.7 0.4 fusion.73
  71.2 0.9 %add_reduce_fusion.5 = f32[16,2048]{1,0:T(8,128)S(1)} fusion(f32[4,16,1,2048]{3,1,2,0:T(8,128)S(1)} %fusion.73, f32[4]{0:T(128)S(1)} %get-tuple-element.527, f32[4]{0:T(128)S(1)} %get-tuple-element.529, f32[4]{0:T(128)S(1)} %get-tuple-element.531, f32[4]{0:T(128)S(1)} %get-tuple-element.532, f32[4]{0:T(128)S(1)} %get-tuple-element.534, ...), kind=kLoop, calls=%fused_computation.105.clone.1 | loop fusion | flops 1802240 | bytes 655472 | tf_op jit(solution)/shard_map/while/body/eval_jaxpr/reduce_sum | solution.py:74
  73.3 0.5 minimum_subtract_fusion.5
  73.8 0.4 fusion.73
  74.2 0.9 %add_reduce_fusion.5 = f32[16,2048]{1,0:T(8,128)S(1)} fusion(f32[4,16,1,2048]{3,1,2,0:T(8,128)S(1)} %fusion.73, f32[4]{0:T(128)S(1)} %get-tuple-element.527, f32[4]{0:T(128)S(1)} %get-tuple-element.529, f32[4]{0:T(128)S(1)} %get-tuple-element.531, f32[4]{0:T(128)S(1)} %get-tuple-element.532, f32[4]{0:T(128)S(1)} %get-tuple-element.534, ...), kind=kLoop, calls=%fused_computation.105.clone.1 | loop fusion | flops 1802240 | bytes 655472 | tf_op jit(solution)/shard_map/while/body/eval_jaxpr/reduce_sum | solution.py:74
  75.4 1.0 %reduce.75 = bf16[16,2048]{1,0:T(8,128)(2,1)S(1)} reduce(bf16[16,1,1,2048]{3,2,1,0:T(2,128)(2,1)S(1)} %bitcast.120, bf16[]{:T(256)} %broadcast.734), dimensions={1,2}, to_apply=%bitcast.99.reduce_sub_computation | reduce | bytes 131074
  76.4 10.1 %all_to_all.40 = bf16[16,2,1024]{2,1,0:T(2,128)(2,1)S(1)} all-to-all(bf16[16,2,1024]{2,1,0:T(2,128)(2,1)S(1)} %reshape.667), channel_id=1, replica_groups=mesh['vessel'=2,'gather'=16] {'gather'}, dimensions={0} | all-to-all | bytes 131072 | tf_op jit(solution)/shard_map/all_to_all | solution.py:104
  86.6 0.7 copy.74
  (90 shorter events, 10.7 us)
Async XLA Ops:
  3.6 0.8 copy-start.1
  4.5 0.8 copy-start
  7.8 8.3 %copy-start.2 = (f32[16,7]{0,1:T(8,128)S(1)}, f32[16,7]{0,1:T(8,128)}, u32[]{:S(2)}) copy-start(f32[16,7]{0,1:T(8,128)} %param.13) | copy-start | bytes 1348
  7.8 15.9 %all-to-all-start = ((bf16[16,2,1024]{2,1,0:T(2,128)(2,1)}), bf16[16,2,1024]{2,1,0:T(2,128)(2,1)S(1)}, u32[]{:S(2)}, u32[]{:S(2)}) async-start(bf16[16,2,1024]{2,1,0:T(2,128)(2,1)} %reshape.661), calls=%async_computation | async-start | bytes 131072 | tf_op jit(solution)/shard_map/all_to_all | solution.py:97
  16.1 0.7 copy-start.3
  16.8 0.7 copy-start.4
  51.7 11.0 %all-to-all-start.2 = ((bf16[16,2,1024]{2,1,0:T(2,128)(2,1)}), bf16[16,2,1024]{2,1,0:T(2,128)(2,1)S(1)}, u32[]{:S(2)}, u32[]{:S(2)}) async-start(bf16[16,2,1024]{2,1,0:T(2,128)(2,1)} %reshape.665), calls=%async_computation.2 | async-start | bytes 131072 | tf_op jit(solution)/shard_map/all_to_all | solution.py:97
